TPU v7x, 32 devices: a whole 2x2x4 slice. The times are simulated.
32 devices in a mesh: col: 8 (over z, x), row: 4 (over y, core).
Axes of the slice: x: 2, y: 2, z: 4, core: 2. Of those that a mesh axis runs over, the one named last changes fastest.
Arguments:
- vorticity: float32 [2, 8, 1024, 2048], P(None, 'row', 'col'), may hold values from -0.0017578125 to 0.0017578125
- divergence: float32 [2, 8, 1024, 2048], P(None, 'row', 'col'), may hold values from -0.0017578125 to 0.0017578125
- trunc_cut: int32 [1024], P('col'), may hold values from -1 to 1023, as said below
- level_slot: int32 [8], replicated, may hold values from 0 to 7, each once
Outputs:
- u_wind: float32 [8, 2048, 2048], P(None, ('col', 'row'))
- v_wind: float32 [8, 2048, 2048], P(None, ('col', 'row'))
- u_slope: float32 [8, 2048, 2048], P(None, ('col', 'row'))
- v_slope: float32 [8, 2048, 2048], P(None, ('col', 'row'))
Inputs may be any that keep to these rules, and one draw needn't show every extreme that they name: trunc_cut never rises with m, is 1023 at m = 0 and -1 (nothing kept) at the last m. level_slot is a permutation of the model levels.
All inputs are finite; a program needn't handle non-finite values.
Results may differ from a plain program's by a relative error of at most 0.0001.
Values sent between devices are 32-bit elements; how exact they have to be, the bound alone decides.
A program may use at most 128 MiB of HBM per device.

v0:
```python
import math

import jax
import jax.numpy as jnp
from jax import lax
from jax.sharding import PartitionSpec as P

HIGHEST = lax.Precision.HIGHEST


def spectral_winds(vorticity, divergence, trunc_cut, first_wave, east_cells):
    local_count = vorticity.shape[2]
    north_cells = vorticity.shape[3]
    wave_index = first_wave + jnp.arange(local_count, dtype=jnp.int32)
    north_index = jnp.arange(north_cells, dtype=jnp.int32)
    north_wave = jnp.where(north_index < north_cells // 2, north_index, north_index - north_cells)
    wave_east = 2.0 * math.pi / east_cells * wave_index.astype(jnp.float32)
    wave_north = 2.0 * math.pi / north_cells * north_wave.astype(jnp.float32)
    east_col = wave_east[:, None]
    north_row = wave_north[None, :]
    square_wave = east_col * east_col + north_row * north_row
    retained = (jnp.abs(north_wave)[None, :] <= trunc_cut[:, None]) & (square_wave > 0)
    inverse_square = jnp.where(retained, 1.0 / jnp.where(square_wave > 0, square_wave, 1.0), 0.0)
    curl_real = vorticity[0]
    curl_imag = vorticity[1]
    source_real = divergence[0]
    source_imag = divergence[1]
    east_real = (-north_row * curl_imag + east_col * source_imag) * inverse_square
    east_imag = (north_row * curl_real - east_col * source_real) * inverse_square
    north_real = (east_col * curl_imag + north_row * source_imag) * inverse_square
    north_imag = (-east_col * curl_real - north_row * source_real) * inverse_square
    return jnp.stack([east_real, east_imag, north_real, north_imag], axis=1)


def north_transform(flattened, local_waves):
    slot_count = flattened.shape[0]
    north_cells = flattened.shape[2]
    block_size = math.gcd(north_cells, 256)
    block_count = north_cells // block_size
    north_index = jnp.arange(north_cells, dtype=jnp.int32)

    def north_one_block(block_index, result):
        row_index = block_index * block_size + jnp.arange(block_size, dtype=jnp.int32)
        phase_steps = row_index[:, None] * north_index[None, :] % north_cells
        angles = 2.0 * math.pi / north_cells * phase_steps.astype(jnp.float32)
        cosine_table = jnp.cos(angles)
        sine_table = jnp.sin(angles)
        with_cosine = jnp.einsum("yn,lkn->lyk", cosine_table, flattened, precision=HIGHEST)
        with_sine = jnp.einsum("yn,lkn->lyk", sine_table, flattened, precision=HIGHEST)
        with_cosine = with_cosine.reshape(slot_count, block_size, 2, 2, local_waves)
        with_sine = with_sine.reshape(slot_count, block_size, 2, 2, local_waves)
        real_part = with_cosine[:, :, :, 0] - with_sine[:, :, :, 1]
        imag_part = with_sine[:, :, :, 0] + with_cosine[:, :, :, 1]
        joined = jnp.concatenate([real_part, imag_part], axis=3)
        return lax.dynamic_update_slice_in_dim(result, joined, block_index * block_size, 1)

    initial = jnp.zeros((slot_count, north_cells, 2, 2 * local_waves), jnp.float32)
    return lax.fori_loop(0, block_count, north_one_block, initial)


def east_transform(stacked, local_waves, east_cells):
    columns = stacked.shape[0]
    slot_count = stacked.shape[1]
    row_count = stacked.shape[2]
    field_count = stacked.shape[3]
    block_size = math.gcd(east_cells, 256)
    block_count = east_cells // block_size
    wave_number = (
        jnp.arange(columns, dtype=jnp.int32)[:, None] * local_waves
        + jnp.arange(local_waves, dtype=jnp.int32)[None, :]
    )
    weights = jnp.where(wave_number == 0, 1.0, 2.0)[:, :, None]
    wave_east = 2.0 * math.pi / east_cells * wave_number.astype(jnp.float32)[:, :, None]

    def east_one_block(block_index, result):
        east_index = block_index * block_size + jnp.arange(block_size, dtype=jnp.int32)
        phase_steps = wave_number[:, :, None] * east_index[None, None, :] % east_cells
        angles = 2.0 * math.pi / east_cells * phase_steps.astype(jnp.float32)
        cosine_table = jnp.cos(angles)
        sine_table = jnp.sin(angles)
        value_real = weights * cosine_table
        value_imag = -weights * sine_table
        slope_real = -weights * wave_east * sine_table
        slope_imag = -weights * wave_east * cosine_table
        value_table = jnp.stack([value_real, value_imag], axis=1)
        slope_table = jnp.stack([slope_real, slope_imag], axis=1)
        east_table = jnp.stack([value_table, slope_table], axis=3).reshape(
            columns, 2 * local_waves, 2, block_size
        )
        product = jnp.einsum("clyfk,ckab->falyb", stacked, east_table, precision=HIGHEST)
        return lax.dynamic_update_slice_in_dim(result, product, block_index * block_size, 4)

    initial = jnp.zeros((field_count, 2, slot_count, row_count, east_cells), jnp.float32)
    return lax.fori_loop(0, block_count, east_one_block, initial)


def place_levels(grid_all, level_slot):
    slot_count = grid_all.shape[2]
    selector = (level_slot[None, :] == jnp.arange(slot_count, dtype=jnp.int32)[:, None]).astype(
        jnp.float32
    )
    return jnp.einsum("ls,fasyx->falyx", selector, grid_all, precision=HIGHEST)


def on_device(vorticity, divergence, trunc_cut, level_slot):
    columns = lax.axis_size("col")
    row_count = lax.axis_size("row")
    local_waves = vorticity.shape[2]
    north_cells = vorticity.shape[3]
    east_cells = 2 * local_waves * columns
    first_wave = lax.axis_index("col") * local_waves
    spectra = spectral_winds(vorticity, divergence, trunc_cut, first_wave, east_cells)
    slot_count = spectra.shape[0]
    flattened = spectra.reshape(slot_count, 4 * local_waves, north_cells)
    fourier = north_transform(flattened, local_waves)
    outgoing = fourier[None]
    received = lax.all_to_all(outgoing, ("col", "row"), split_axis=2, concat_axis=0, tiled=True)
    shaped = received.reshape(
        columns,
        row_count * received.shape[1],
        received.shape[2],
        received.shape[3],
        received.shape[4],
    )
    grid_all = east_transform(shaped, local_waves, east_cells)
    placed = place_levels(grid_all, level_slot)
    return (placed[0, 0], placed[1, 0], placed[0, 1], placed[1, 1])


def solution(mesh):
    return jax.shard_map(
        on_device,
        mesh=mesh,
        in_specs=(P(None, "row", "col", None), P(None, "row", "col", None), P("col"), P()),
        out_specs=(
            P(None, ("col", "row"), None),
            P(None, ("col", "row"), None),
            P(None, ("col", "row"), None),
            P(None, ("col", "row"), None),
        ),
        check_vma=False,
    )
```

profile of v0, /device:TPU:6, one launch (start us, length us, event | category | flops | bytes accessed | tf_op | source)
XLA Modules:
  0.0 820.9 jit_solution(6526795939070336605)
XLA Ops:
  1.7 4.5 fusion.57
  6.8 3.8 copy.46
  10.6 5.5 broadcast_in_dim.32.clone
  16.1 356.5 %while.35 = (s32[]{:T(128)}, f32[2,2048,2,256]{3,2,0,1:T(2,128)}, f32[2,512,2048]{2,1,0:T(8,128)}, s32[]{:T(128)}, s32[]{:T(128)}, /*index=5*/s32[]{:T(128)}, s32[]{:T(128)}) while((s32[]{:T(128)}, f32[2,2048,2,256]{3,2,0,1:T(2,128)}, f32[2,512,2048]{2,1,0:T(8,128)}, s32[]{:T(128)}, s32[]{:T(128)}, /*index=5*/s32[]{:T(128)}, ...), condition=%wide.region_1.2_spmd.clone, body=%wide.region_0.1_spmd.clone.sunk | while | flops 12900106240 | bytes 32509060 | solution.py:58
  38.5 18.1 %fusion.96 = f32[2,256,512]{2,1,0:T(8,128)S(1)} fusion(f32[2,512,2048]{2,1,0:T(8,128)} %get-tuple-element.528, s32[256]{0:T(256)S(1)} %iota_add_fusion.7), kind=kOutput, calls=%fused_computation.21.clone.1 | convolution fusion | flops 6449790976 | bytes 9438208 | tf_op jit(solution)/shard_map/while/body/eval_jaxpr/yn,lkn->lyk/dot_general | solution.py:48
  58.1 18.2 %fusion.94 = f32[2,256,512]{2,1,0:T(8,128)S(1)} fusion(f32[2,512,2048]{2,1,0:T(8,128)} %get-tuple-element.528, s32[256]{0:T(256)S(1)} %iota_add_fusion.7), kind=kOutput, calls=%fused_computation.22.clone.1 | convolution fusion | flops 6449790976 | bytes 9438208 | tf_op jit(solution)/shard_map/while/body/eval_jaxpr/yn,lkn->lyk/dot_general | solution.py:49
  79.9 18.1 %fusion.96 = f32[2,256,512]{2,1,0:T(8,128)S(1)} fusion(f32[2,512,2048]{2,1,0:T(8,128)} %get-tuple-element.528, s32[256]{0:T(256)S(1)} %iota_add_fusion.7), kind=kOutput, calls=%fused_computation.21.clone.1 | convolution fusion | flops 6449790976 | bytes 9438208 | tf_op jit(solution)/shard_map/while/body/eval_jaxpr/yn,lkn->lyk/dot_general | solution.py:48
  99.5 18.2 %fusion.94 = f32[2,256,512]{2,1,0:T(8,128)S(1)} fusion(f32[2,512,2048]{2,1,0:T(8,128)} %get-tuple-element.528, s32[256]{0:T(256)S(1)} %iota_add_fusion.7), kind=kOutput, calls=%fused_computation.22.clone.1 | convolution fusion | flops 6449790976 | bytes 9438208 | tf_op jit(solution)/shard_map/while/body/eval_jaxpr/yn,lkn->lyk/dot_general | solution.py:49
  121.1 18.1 %fusion.96 = f32[2,256,512]{2,1,0:T(8,128)S(1)} fusion(f32[2,512,2048]{2,1,0:T(8,128)} %get-tuple-element.528, s32[256]{0:T(256)S(1)} %iota_add_fusion.7), kind=kOutput, calls=%fused_computation.21.clone.1 | convolution fusion | flops 6449790976 | bytes 9438208 | tf_op jit(solution)/shard_map/while/body/eval_jaxpr/yn,lkn->lyk/dot_general | solution.py:48
  140.7 18.2 %fusion.94 = f32[2,256,512]{2,1,0:T(8,128)S(1)} fusion(f32[2,512,2048]{2,1,0:T(8,128)} %get-tuple-element.528, s32[256]{0:T(256)S(1)} %iota_add_fusion.7), kind=kOutput, calls=%fused_computation.22.clone.1 | convolution fusion | flops 6449790976 | bytes 9438208 | tf_op jit(solution)/shard_map/while/body/eval_jaxpr/yn,lkn->lyk/dot_general | solution.py:49
  162.4 18.1 %fusion.96 = f32[2,256,512]{2,1,0:T(8,128)S(1)} fusion(f32[2,512,2048]{2,1,0:T(8,128)} %get-tuple-element.528, s32[256]{0:T(256)S(1)} %iota_add_fusion.7), kind=kOutput, calls=%fused_computation.21.clone.1 | convolution fusion | flops 6449790976 | bytes 9438208 | tf_op jit(solution)/shard_map/while/body/eval_jaxpr/yn,lkn->lyk/dot_general | solution.py:48
  182.0 18.2 %fusion.94 = f32[2,256,512]{2,1,0:T(8,128)S(1)} fusion(f32[2,512,2048]{2,1,0:T(8,128)} %get-tuple-element.528, s32[256]{0:T(256)S(1)} %iota_add_fusion.7), kind=kOutput, calls=%fused_computation.22.clone.1 | convolution fusion | flops 6449790976 | bytes 9438208 | tf_op jit(solution)/shard_map/while/body/eval_jaxpr/yn,lkn->lyk/dot_general | solution.py:49
  203.7 18.1 %fusion.96 = f32[2,256,512]{2,1,0:T(8,128)S(1)} fusion(f32[2,512,2048]{2,1,0:T(8,128)} %get-tuple-element.528, s32[256]{0:T(256)S(1)} %iota_add_fusion.7), kind=kOutput, calls=%fused_computation.21.clone.1 | convolution fusion | flops 6449790976 | bytes 9438208 | tf_op jit(solution)/shard_map/while/body/eval_jaxpr/yn,lkn->lyk/dot_general | solution.py:48
  223.3 18.2 %fusion.94 = f32[2,256,512]{2,1,0:T(8,128)S(1)} fusion(f32[2,512,2048]{2,1,0:T(8,128)} %get-tuple-element.528, s32[256]{0:T(256)S(1)} %iota_add_fusion.7), kind=kOutput, calls=%fused_computation.22.clone.1 | convolution fusion | flops 6449790976 | bytes 9438208 | tf_op jit(solution)/shard_map/while/body/eval_jaxpr/yn,lkn->lyk/dot_general | solution.py:49
  245.1 18.1 %fusion.96 = f32[2,256,512]{2,1,0:T(8,128)S(1)} fusion(f32[2,512,2048]{2,1,0:T(8,128)} %get-tuple-element.528, s32[256]{0:T(256)S(1)} %iota_add_fusion.7), kind=kOutput, calls=%fused_computation.21.clone.1 | convolution fusion | flops 6449790976 | bytes 9438208 | tf_op jit(solution)/shard_map/while/body/eval_jaxpr/yn,lkn->lyk/dot_general | solution.py:48
  264.7 18.2 %fusion.94 = f32[2,256,512]{2,1,0:T(8,128)S(1)} fusion(f32[2,512,2048]{2,1,0:T(8,128)} %get-tuple-element.528, s32[256]{0:T(256)S(1)} %iota_add_fusion.7), kind=kOutput, calls=%fused_computation.22.clone.1 | convolution fusion | flops 6449790976 | bytes 9438208 | tf_op jit(solution)/shard_map/while/body/eval_jaxpr/yn,lkn->lyk/dot_general | solution.py:49
  286.4 18.1 %fusion.96 = f32[2,256,512]{2,1,0:T(8,128)S(1)} fusion(f32[2,512,2048]{2,1,0:T(8,128)} %get-tuple-element.528, s32[256]{0:T(256)S(1)} %iota_add_fusion.7), kind=kOutput, calls=%fused_computation.21.clone.1 | convolution fusion | flops 6449790976 | bytes 9438208 | tf_op jit(solution)/shard_map/while/body/eval_jaxpr/yn,lkn->lyk/dot_general | solution.py:48
  306.0 18.2 %fusion.94 = f32[2,256,512]{2,1,0:T(8,128)S(1)} fusion(f32[2,512,2048]{2,1,0:T(8,128)} %get-tuple-element.528, s32[256]{0:T(256)S(1)} %iota_add_fusion.7), kind=kOutput, calls=%fused_computation.22.clone.1 | convolution fusion | flops 6449790976 | bytes 9438208 | tf_op jit(solution)/shard_map/while/body/eval_jaxpr/yn,lkn->lyk/dot_general | solution.py:49
  327.7 18.1 %fusion.96 = f32[2,256,512]{2,1,0:T(8,128)S(1)} fusion(f32[2,512,2048]{2,1,0:T(8,128)} %get-tuple-element.528, s32[256]{0:T(256)S(1)} %iota_add_fusion.7), kind=kOutput, calls=%fused_computation.21.clone.1 | convolution fusion | flops 6449790976 | bytes 9438208 | tf_op jit(solution)/shard_map/while/body/eval_jaxpr/yn,lkn->lyk/dot_general | solution.py:48
  347.3 18.2 %fusion.94 = f32[2,256,512]{2,1,0:T(8,128)S(1)} fusion(f32[2,512,2048]{2,1,0:T(8,128)} %get-tuple-element.528, s32[256]{0:T(256)S(1)} %iota_add_fusion.7), kind=kOutput, calls=%fused_computation.22.clone.1 | convolution fusion | flops 6449790976 | bytes 9438208 | tf_op jit(solution)/shard_map/while/body/eval_jaxpr/yn,lkn->lyk/dot_general | solution.py:49
  372.6 6.1 all-to-all-start
  378.7 188.5 %all-to-all-done = f32[1,2,2048,2,256]{4,3,1,0,2:T(2,128)} async-done(((f32[1,2,2048,2,256]{4,3,1,0,2:T(2,128)}), f32[1,2,2048,2,256]{4,3,1,0,2:T(2,128)}, u32[]{:S(2)}, u32[]{:S(2)}) %all-to-all-start) | async-done | bytes 8388640 | tf_op jit(solution)/shard_map/all_to_all | solution.py:117
  567.2 5.0 copy.48
  573.3 3.8 copy.50
  577.2 7.9 broadcast_in_dim.27.clone
  585.0 192.5 %while.36 = (s32[]{:T(128)}, f32[2,2,8,64,2048]{4,2,3,1,0:T(8,128)}, f32[8,8,64,2,256]{4,2,0,3,1:T(8,128)}, s32[8]{0:T(128)S(1)}, s32[]{:T(128)}, /*index=5*/s32[]{:T(128)}, s32[]{:T(128)}, s32[]{:T(128)}) while((s32[]{:T(128)}, f32[2,2,8,64,2048]{4,2,3,1,0:T(8,128)}, f32[8,8,64,2,256]{4,2,0,3,1:T(8,128)}, ...), condition=%wide.region_3.4_spmd.clone.clone.clone, body=%wide.region_2.3_spmd.clone.clone.clone.sunk | while | flops 12891725824 | bytes 65046760 | solution.py:94
  585.6 4.3 broadcast_multiply_fusion.4
  590.3 2.9 copy-done
  593.3 13.6 %fusion.99 = f32[2,2,8,64,256]{4,3,0,2,1:T(8,128)S(1)} fusion(f32[8,8,64,2,256]{4,2,0,3,1:T(8,128)S(1)} %copy-done, f32[8,256,1,256]{3,1,0,2:T(8,128)S(1)} %bitcast.142, f32[8,256,1,256]{3,1,0,2:T(8,128)S(1)} %bitcast.141), kind=kOutput, calls=%fused_computation.47.clone.1 | convolution fusion | flops 12885950464 | bytes 14680064 | tf_op jit(solution)/shard_map/while/body/eval_jaxpr/clyfk,ckab->falyb/dot_general | solution.py:90
  606.8 2.6 copy_dynamic-update-slice_fusion.5
  609.6 4.3 broadcast_multiply_fusion.4
  614.4 2.9 copy-done
  617.3 13.5 %fusion.99 = f32[2,2,8,64,256]{4,3,0,2,1:T(8,128)S(1)} fusion(f32[8,8,64,2,256]{4,2,0,3,1:T(8,128)S(1)} %copy-done, f32[8,256,1,256]{3,1,0,2:T(8,128)S(1)} %bitcast.142, f32[8,256,1,256]{3,1,0,2:T(8,128)S(1)} %bitcast.141), kind=kOutput, calls=%fused_computation.47.clone.1 | convolution fusion | flops 12885950464 | bytes 14680064 | tf_op jit(solution)/shard_map/while/body/eval_jaxpr/clyfk,ckab->falyb/dot_general | solution.py:90
  630.8 2.6 copy_dynamic-update-slice_fusion.5
  633.6 4.3 broadcast_multiply_fusion.4
  638.3 2.9 copy-done
  641.3 13.5 %fusion.99 = f32[2,2,8,64,256]{4,3,0,2,1:T(8,128)S(1)} fusion(f32[8,8,64,2,256]{4,2,0,3,1:T(8,128)S(1)} %copy-done, f32[8,256,1,256]{3,1,0,2:T(8,128)S(1)} %bitcast.142, f32[8,256,1,256]{3,1,0,2:T(8,128)S(1)} %bitcast.141), kind=kOutput, calls=%fused_computation.47.clone.1 | convolution fusion | flops 12885950464 | bytes 14680064 | tf_op jit(solution)/shard_map/while/body/eval_jaxpr/clyfk,ckab->falyb/dot_general | solution.py:90
  654.8 2.6 copy_dynamic-update-slice_fusion.5
  657.6 4.3 broadcast_multiply_fusion.4
  662.3 2.9 copy-done
  665.2 13.6 %fusion.99 = f32[2,2,8,64,256]{4,3,0,2,1:T(8,128)S(1)} fusion(f32[8,8,64,2,256]{4,2,0,3,1:T(8,128)S(1)} %copy-done, f32[8,256,1,256]{3,1,0,2:T(8,128)S(1)} %bitcast.142, f32[8,256,1,256]{3,1,0,2:T(8,128)S(1)} %bitcast.141), kind=kOutput, calls=%fused_computation.47.clone.1 | convolution fusion | flops 12885950464 | bytes 14680064 | tf_op jit(solution)/shard_map/while/body/eval_jaxpr/clyfk,ckab->falyb/dot_general | solution.py:90
  678.8 2.6 copy_dynamic-update-slice_fusion.5
  681.5 4.3 broadcast_multiply_fusion.4
  686.3 2.9 copy-done
  689.2 13.6 %fusion.99 = f32[2,2,8,64,256]{4,3,0,2,1:T(8,128)S(1)} fusion(f32[8,8,64,2,256]{4,2,0,3,1:T(8,128)S(1)} %copy-done, f32[8,256,1,256]{3,1,0,2:T(8,128)S(1)} %bitcast.142, f32[8,256,1,256]{3,1,0,2:T(8,128)S(1)} %bitcast.141), kind=kOutput, calls=%fused_computation.47.clone.1 | convolution fusion | flops 12885950464 | bytes 14680064 | tf_op jit(solution)/shard_map/while/body/eval_jaxpr/clyfk,ckab->falyb/dot_general | solution.py:90
  702.8 2.6 copy_dynamic-update-slice_fusion.5
  705.6 4.3 broadcast_multiply_fusion.4
  710.3 2.9 copy-done
  713.2 13.6 %fusion.99 = f32[2,2,8,64,256]{4,3,0,2,1:T(8,128)S(1)} fusion(f32[8,8,64,2,256]{4,2,0,3,1:T(8,128)S(1)} %copy-done, f32[8,256,1,256]{3,1,0,2:T(8,128)S(1)} %bitcast.142, f32[8,256,1,256]{3,1,0,2:T(8,128)S(1)} %bitcast.141), kind=kOutput, calls=%fused_computation.47.clone.1 | convolution fusion | flops 12885950464 | bytes 14680064 | tf_op jit(solution)/shard_map/while/body/eval_jaxpr/clyfk,ckab->falyb/dot_general | solution.py:90
  726.8 2.6 copy_dynamic-update-slice_fusion.5
  729.6 4.3 broadcast_multiply_fusion.4
  734.3 2.9 copy-done
  737.2 13.6 %fusion.99 = f32[2,2,8,64,256]{4,3,0,2,1:T(8,128)S(1)} fusion(f32[8,8,64,2,256]{4,2,0,3,1:T(8,128)S(1)} %copy-done, f32[8,256,1,256]{3,1,0,2:T(8,128)S(1)} %bitcast.142, f32[8,256,1,256]{3,1,0,2:T(8,128)S(1)} %bitcast.141), kind=kOutput, calls=%fused_computation.47.clone.1 | convolution fusion | flops 12885950464 | bytes 14680064 | tf_op jit(solution)/shard_map/while/body/eval_jaxpr/clyfk,ckab->falyb/dot_general | solution.py:90
  750.8 2.6 copy_dynamic-update-slice_fusion.5
  753.6 4.3 broadcast_multiply_fusion.4
  758.3 2.9 copy-done
  761.2 13.6 %fusion.99 = f32[2,2,8,64,256]{4,3,0,2,1:T(8,128)S(1)} fusion(f32[8,8,64,2,256]{4,2,0,3,1:T(8,128)S(1)} %copy-done, f32[8,256,1,256]{3,1,0,2:T(8,128)S(1)} %bitcast.142, f32[8,256,1,256]{3,1,0,2:T(8,128)S(1)} %bitcast.141), kind=kOutput, calls=%fused_computation.47.clone.1 | convolution fusion | flops 12885950464 | bytes 14680064 | tf_op jit(solution)/shard_map/while/body/eval_jaxpr/clyfk,ckab->falyb/dot_general | solution.py:90
  774.8 2.6 copy_dynamic-update-slice_fusion.5
  777.6 19.0 %convolution_bitcast_fusion = f32[2,2,8,64,2048]{4,2,3,1,0:T(8,128)} fusion(f32[2,2,8,64,2048]{4,2,3,1,0:T(8,128)} %get-tuple-element.306, s32[8]{0:T(128)S(1)} %copy-done.1), kind=kOutput, calls=%fused_computation.70 | convolution fusion | flops 402653248 | bytes 33554464 | tf_op jit(solution)/shard_map/ls,fasyx->falyx/dot_general | solution.py:102
  796.5 6.5 slice_bitcast_fusion
  803.0 4.4 copy.55
  807.4 4.4 copy.54
  811.9 4.4 copy.53
  816.3 4.4 copy.52
  (107 shorter events, 47.5 us)
Async XLA Ops:
  372.6 194.6 %all-to-all-start = ((f32[1,2,2048,2,256]{4,3,1,0,2:T(2,128)}), f32[1,2,2048,2,256]{4,3,1,0,2:T(2,128)}, u32[]{:S(2)}, u32[]{:S(2)}) async-start(f32[1,2,2048,2,256]{4,3,1,0,2:T(2,128)} %bitcast.147), calls=%async_computation | async-start | bytes 16777216 | tf_op jit(solution)/shard_map/all_to_all | solution.py:117
  585.0 192.5 %copy-start.1 = (s32[8]{0:T(128)S(1)}, s32[8]{0:T(128)}, u32[]{:S(2)}) copy-start(s32[8]{0:T(128)} %param.11) | copy-start | bytes 100
  589.9 3.4 copy-start
  613.9 3.4 copy-start
  637.9 3.4 copy-start
  661.8 3.4 copy-start
  685.8 3.4 copy-start
  709.8 3.4 copy-start
  733.8 3.4 copy-start
  757.9 3.4 copy-start
where the time goes:
time: 824 us; the launch traced here: 821 us
  matrix products  417 us (51%)
  waiting for transfers between devices  188 us (23%)
  local copies, waits for them, and re-layouts  119 us (14%)
  other arithmetic  61.3 us (7%)
  loops' own time  27.3 us (3%)
    all_to_all x1, waiting for transfers between devices, on_device(): lax.all_to_all(outgoing, ('col', 'row'), split_axis=2, concat_axis=0, til...  188 us
    dot_general x8, matrix products, north_one_block(): jnp.einsum('yn,lkn->lyk', sine_table, flattened, precision=HIGHEST)  145 us
    dot_general x8, matrix products, north_one_block(): jnp.einsum('yn,lkn->lyk', cosine_table, flattened, precision=HIGHEST)  145 us
    dot_general x8, matrix products, east_one_block(): jnp.einsum('clyfk,ckab->falyb', stacked, east_table, precision=HIGHEST)  108 us
    mul x8, other arithmetic, east_one_block(): slope_real = -weights * wave_east * sine_table  34.2 us
    another operation x1, loops' own time, north_transform(): return lax.fori_loop(0, block_count, north_one_block, initial)  26.5 us
    while x16, local copies, waits for them, and re-layouts  23.4 us
    unnamed x7, local copies, waits for them, and re-layouts  21.6 us
  transfers between devices with their start and end apart: 1, of which 1 were waited for; matrix products, arithmetic and copies ran while one was open for 0% of the time, Pallas kernels for 0%

commit v1 on v0

v1 whole, which is shorter than its diff:
```python
import math

import jax
import jax.numpy as jnp
import numpy as np
from jax import lax
from jax.sharding import PartitionSpec as P

HIGH = lax.Precision.HIGH


def split_waves(array, axis):
    first = lax.slice_in_dim(array, 0, None, 2, axis)
    second = lax.slice_in_dim(array, 1, None, 2, axis)
    return jnp.concatenate([first, second], axis)


def phases(product, period):
    angles = 2.0 * np.pi * (product % period) / period
    return np.cos(angles).astype(np.float32), np.sin(angles).astype(np.float32)


def multiply(first, second):
    return first[0] * second[0] - first[1] * second[1], first[0] * second[1] + first[1] * second[0]


def north_table(north_cells):
    quarter = north_cells // 4
    fine = math.gcd(quarter, 32)
    column = np.arange(quarter)
    coarse_row = 4 * fine * np.arange(quarter // fine)[None, :, None, None] + np.arange(4)[:, None, None, None]
    fine_row = 4 * np.arange(fine)[None, None, :, None]
    coarse = phases(coarse_row * column, north_cells)
    close = phases(fine_row * column, north_cells)
    coarse, close = lax.optimization_barrier((coarse, close))
    cosine, sine = multiply(coarse, close)
    joined = jnp.concatenate([cosine, -sine], axis=3)
    return joined.reshape(4, quarter, 2 * quarter)


def east_table(columns, local_waves, east_cells):
    half = local_waves // 2
    cells = east_cells // 2
    column = np.arange(cells)
    coarse_wave = np.arange(2)[:, None, None, None] + local_waves * np.arange(columns)[None, :, None, None]
    close_wave = 2 * np.arange(half)[None, None, :, None]
    coarse = phases(coarse_wave * column, east_cells)
    close = phases(close_wave * column, east_cells)
    coarse, close = lax.optimization_barrier((coarse, close))
    cosine, sine = multiply(coarse, close)
    wave = coarse_wave + close_wave
    weights = np.where(wave == 0, 1.0, 2.0).astype(np.float32)
    scaled = (weights * wave * (2.0 * np.pi / east_cells)).astype(np.float32)
    real = jnp.concatenate([weights * cosine, -scaled * sine], axis=3)
    imag = jnp.concatenate([-weights * sine, -scaled * cosine], axis=3)
    joined = jnp.stack([real, imag], axis=2)
    return joined.reshape(2, columns * local_waves, 2 * cells)


def spectral_winds(vorticity, divergence, trunc_cut, wave_index, east_cells):
    north_cells = vorticity.shape[3]
    north_index = jnp.arange(north_cells, dtype=jnp.int32)
    north_wave = jnp.where(north_index < north_cells // 2, north_index, north_index - north_cells)
    wave_east = 2.0 * math.pi / east_cells * wave_index.astype(jnp.float32)
    wave_north = 2.0 * math.pi / north_cells * north_wave.astype(jnp.float32)
    east_col = wave_east[:, None]
    north_row = wave_north[None, :]
    square_wave = east_col * east_col + north_row * north_row
    retained = (jnp.abs(north_wave)[None, :] <= trunc_cut[:, None]) & (square_wave > 0)
    inverse_square = jnp.where(retained, 1.0 / jnp.where(square_wave > 0, square_wave, 1.0), 0.0)
    east_inverse = east_col * inverse_square
    north_inverse = north_row * inverse_square
    curl_real, curl_imag = vorticity[0], vorticity[1]
    source_real, source_imag = divergence[0], divergence[1]
    east = (
        -north_inverse * curl_imag + east_inverse * source_imag,
        north_inverse * curl_real - east_inverse * source_real,
    )
    north = (
        east_inverse * curl_imag + north_inverse * source_imag,
        -east_inverse * curl_real - north_inverse * source_real,
    )
    return east, north


def fold_quarters(wind, slots, half):
    real, imag = wind
    quarter = real.shape[2] // 4
    r0, r1, r2, r3 = (real[:, :, q * quarter:(q + 1) * quarter] for q in range(4))
    i0, i1, i2, i3 = (imag[:, :, q * quarter:(q + 1) * quarter] for q in range(4))
    folded = (
        (r0 + r2 + (r1 + r3), i0 + i2 + (i1 + i3)),
        (r0 - r2 - (i1 - i3), i0 - i2 + (r1 - r3)),
        (r0 + r2 - (r1 + r3), i0 + i2 - (i1 + i3)),
        (r0 - r2 + (i1 - i3), i0 - i2 - (r1 - r3)),
    )
    parts = []
    for part_real, part_imag in folded:
        shape = (slots, 2, 1, half, 2 * quarter)
        top = jnp.concatenate([part_real, part_imag], axis=2).reshape(shape)
        low = jnp.concatenate([part_imag, -part_real], axis=2).reshape(shape)
        parts.append(jnp.concatenate([top, low], axis=2))
    return jnp.stack(parts, axis=0).reshape(4, slots * 4 * half, 2 * quarter)


def on_device(vorticity, divergence, trunc_cut, level_slot):
    columns = lax.axis_size("col")
    row_devices = lax.axis_size("row")
    slots, local_waves, north_cells = vorticity.shape[1:]
    half = local_waves // 2
    quarter = north_cells // 4
    levels = slots * row_devices
    east_cells = 2 * local_waves * columns
    cells = east_cells // 2
    block = quarter // (columns * row_devices)
    first_wave = lax.axis_index("col") * local_waves
    wave_index = first_wave + jnp.arange(local_waves, dtype=jnp.int32)
    winds = spectral_winds(
        split_waves(vorticity, 2),
        split_waves(divergence, 2),
        split_waves(trunc_cut, 0),
        split_waves(wave_index, 0),
        east_cells,
    )
    table_north = north_table(north_cells)
    table_east = east_table(columns, local_waves, east_cells)
    holder = jnp.argsort(level_slot).astype(jnp.int32)
    results = []
    for wind in winds:
        folded = fold_quarters(wind, slots, half)
        fourier = jnp.einsum("pjk,pmk->pjm", table_north, folded, precision=HIGH)
        outgoing = fourier.reshape(4, quarter, slots, 2 * local_waves).transpose(1, 2, 0, 3)
        received = lax.all_to_all(outgoing, ("col", "row"), split_axis=0, concat_axis=0, tiled=True)
        shaped = received.reshape(columns, row_devices, block, slots, 4, 2, local_waves)
        arranged = shaped.transpose(1, 3, 5, 2, 4, 0, 6).reshape(
            levels, 2, block * 4, columns * local_waves
        )
        placed = jnp.concatenate(
            [lax.dynamic_slice_in_dim(arranged, holder[level], 1, 0) for level in range(levels)], axis=0
        )
        even = jnp.einsum("lyk,kx->lyx", placed[:, 0], table_east[0], precision=HIGH)
        odd = jnp.einsum("lyk,kx->lyx", placed[:, 1], table_east[1], precision=HIGH)
        total, rest = even + odd, even - odd
        results.append(
            (
                jnp.concatenate([total[:, :, :cells], rest[:, :, :cells]], axis=2),
                jnp.concatenate([total[:, :, cells:], rest[:, :, cells:]], axis=2),
            )
        )
    return results[0][0], results[1][0], results[0][1], results[1][1]


def solution(mesh):
    return jax.shard_map(
        on_device,
        mesh=mesh,
        in_specs=(P(None, "row", "col", None), P(None, "row", "col", None), P("col"), P()),
        out_specs=(
            P(None, ("col", "row"), None),
            P(None, ("col", "row"), None),
            P(None, ("col", "row"), None),
            P(None, ("col", "row"), None),
        ),
        check_vma=False,
    )
```

time: 824 us -> 373 us (0.45)
  matrix products: 417 us -> 66.9 us
  waiting for transfers between devices: 188 us -> 102 us
  loops' own time: 27.3 us -> 0 us
  between operations: 0.94 us -> 16.5 us
  local copies, waits for them, and re-layouts: 119 us -> 109 us
    dot_general x25 -> x6, matrix products: 417 us -> 66.9 us  [the longest x2 28.6 us: on_device(): fourier = jnp.einsum('pjk,pmk->pjm', table_north, folded, precision=HIGH)]
    all_to_all x1 -> x2, waiting for transfers between devices: 188 us -> 102 us  [on_device(): lax.all_to_all(outgoing, ('col', 'row'), split_axis=0, concat_axis=0, til...]
    mul x19 -> x1, other arithmetic: 39.3 us -> 5.38 us  [east_table(): imag = jnp.concatenate([-weights * sine, -scaled * cosine], axis=3)]
    slice x16 -> x13, local copies, waits for them, and re-layouts: 13 us -> 44.7 us  [the longest x4 20.8 us: split_waves(): first = lax.slice_in_dim(array, 0, None, 2, axis)]
    another operation x2 -> x0, loops' own time: 27.3 us -> none  [the longest x1 26.5 us: north_transform(): return lax.fori_loop(0, block_count, north_one_block, initial)]
    concatenate x0 -> x21, other arithmetic: none -> 24.1 us  [the longest x8 11.9 us: fold_quarters(): parts.append(jnp.concatenate([top, low], axis=2))]
    while x16 -> x0, local copies, waits for them, and re-layouts: 23.4 us -> none
    reshape x16 -> x6, local copies, waits for them, and re-layouts: 10.8 us -> 33.2 us  [the longest x2 12.5 us: on_device(): received.reshape(columns, row_devices, block, slots, 4, 2, local_waves)]
  transfers between devices with their start and end apart: 1 -> 2, of which waited for: 1 -> 2; matrix products, arithmetic and copies ran while one was open for 0% -> 19% of each run, Pallas kernels for 0% -> 0%
where the time goes in v1:
time: 373 us; the launch traced here: 366 us
  local copies, waits for them, and re-layouts  109 us (29%)
  waiting for transfers between devices  102 us (27%)
  matrix products  66.9 us (18%)
  other arithmetic  59 us (16%)
  between operations  16.5 us (4%)
  starting transfers between devices  12.9 us (3%)
    all_to_all x2, waiting for transfers between devices, on_device(): lax.all_to_all(outgoing, ('col', 'row'), split_axis=0, concat_axis=0, til...  102 us
    dot_general x2, matrix products, on_device(): fourier = jnp.einsum('pjk,pmk->pjm', table_north, folded, precision=HIGH)  28.6 us
    dot_general x2, matrix products, on_device(): jnp.einsum('lyk,kx->lyx', placed[:, 0], table_east[0], precision=HIGH)  23.2 us
    slice x4, local copies, waits for them, and re-layouts, split_waves(): first = lax.slice_in_dim(array, 0, None, 2, axis)  20.8 us
    slice x4, local copies, waits for them, and re-layouts, split_waves(): second = lax.slice_in_dim(array, 1, None, 2, axis)  18.9 us
    unnamed x70, local copies, waits for them, and re-layouts  17.4 us
    another operation x2, other arithmetic, east_table(): joined = jnp.stack([real, imag], axis=2)  16.2 us
    dot_general x2, matrix products, on_device(): odd = jnp.einsum('lyk,kx->lyx', placed[:, 1], table_east[1], precision=HIGH)  15.1 us
  transfers between devices with their start and end apart: 2, of which 2 were waited for; matrix products, arithmetic and copies ran while one was open for 19% of the time, Pallas kernels for 0%

profile of v1, /device:TPU:6, one launch (start us, length us, event | category | flops | bytes accessed | tf_op | source)
XLA Modules:
  0.0 365.8 jit_solution(9012250437534499265)
XLA Ops:
  0.6 0.8 slice.163
  1.4 0.8 slice.162
  2.6 8.1 %slice.167 = f32[2,2,64,2048]{3,2,1,0:T(8,128)S(1)} slice(f32[2,2,128,2048]{3,2,1,0:T(8,128)} %param.16), slice={[0:2:1], [0:2:1], [1:128:2], [0:2048:1]} | slice | bytes 4194304 | tf_op jit(solution)/shard_map/slice | solution.py:14
  10.7 10.0 %slice.166 = f32[2,2,64,2048]{3,2,1,0:T(8,128)} slice(f32[2,2,128,2048]{3,2,1,0:T(8,128)} %param.16), slice={[0:2:1], [0:2:1], [0:128:2], [0:2048:1]} | slice | bytes 4194304 | tf_op jit(solution)/shard_map/slice | solution.py:13
  20.8 9.8 %slice.170 = f32[2,2,64,2048]{3,2,1,0:T(8,128)} slice(f32[2,2,128,2048]{3,2,1,0:T(8,128)} %param.17), slice={[0:2:1], [0:2:1], [1:128:2], [0:2048:1]} | slice | bytes 4194304 | tf_op jit(solution)/shard_map/slice | solution.py:14
  30.6 9.8 %slice.169 = f32[2,2,64,2048]{3,2,1,0:T(8,128)} slice(f32[2,2,128,2048]{3,2,1,0:T(8,128)} %param.17), slice={[0:2:1], [0:2:1], [0:128:2], [0:2048:1]} | slice | bytes 4194304 | tf_op jit(solution)/shard_map/slice | solution.py:13
  40.6 0.5 fusion.53
  41.1 0.9 copy-done.3
  42.0 0.6 copy-done.4
  42.6 2.0 multiply_subtract_fusion.1
  44.9 1.3 copy-done.2
  46.2 2.9 multiply_add_fusion.1
  49.1 0.6 fusion.50
  49.7 0.3 fusion.60
  50.3 1.5 pad_maximum_fusion.14
  52.1 1.5 pad_maximum_fusion.15
  53.9 1.5 pad_maximum_fusion.16
  55.6 1.5 pad_maximum_fusion.17
  57.4 4.6 %fusion.17 = (f32[4,512,512]{2,1,0:T(8,128)}, f32[4,512,512]{2,1,0:T(8,128)}) fusion(f32[512,512]{1,0:T(8,128)S(1)} %bitcast.193, f32[4,16,512]{2,1,0:T(8,128)S(1)} %bitcast.204, f32[512,512]{1,0:T(8,128)S(1)} %bitcast.192, f32[4,16,512]{2,1,0:T(8,128)S(1)} %bitcast.205), kind=kLoop, calls=%fused_computation.27 | loop fusion | flops 7340032 | bytes 10747904 | tf_op jit(solution)/shard_map/sub | solution.py:24
  62.0 14.6 %fusion.9 = f32[4,512,512]{1,2,0:T(8,128)} fusion(f32[1,512,1024]{2,1,0:T(8,128)} %bitcast.199, f32[1,512,1024]{2,1,0:T(8,128)} %bitcast.198, f32[1,512,1024]{2,1,0:T(8,128)} %bitcast.196, f32[1,512,1024]{2,1,0:T(8,128)} %bitcast.194, f32[4,512,512]{2,1,0:T(8,128)} %get-tuple-element.70, f32[4,512,512]{2,1,0:T(8,128)} %get-tuple-element.69), kind=kOutput, calls=%fused_computation.15 | convolution fusion | flops 6450839552 | bytes 20971520 | tf_op jit(solution)/shard_map/pjk,pmk->pjm/dot_general | solution.py:131
  76.6 5.4 %copy.80 = f32[4,512,2,256]{3,0,2,1:T(4,128)} copy(f32[4,512,2,256]{1,3,2,0:T(8,128)} %bitcast.175) | data formatting | bytes 8388608 | tf_op jit(solution)/shard_map/reshape | solution.py:132
  82.0 6.5 %all-to-all-start.1 = ((f32[512,2,4,256]{3,2,1,0:T(4,128)}), f32[512,2,4,256]{3,2,1,0:T(4,128)}, u32[]{:S(2)}, u32[]{:S(2)}) async-start(f32[512,2,4,256]{3,2,1,0:T(4,128)} %bitcast.171), calls=%async_computation.1 | async-start | bytes 8388608 | tf_op jit(solution)/shard_map/all_to_all | solution.py:133
  88.8 1.4 copy-done
  90.6 1.5 pad_maximum_fusion.10
  92.1 0.5 fusion.42
  92.9 1.5 pad_maximum_fusion.11
  94.7 1.5 pad_maximum_fusion.12
  96.5 1.5 pad_maximum_fusion.13
  98.3 14.0 %fusion.1 = f32[4,512,512]{1,2,0:T(8,128)} fusion(f32[1,512,1024]{2,1,0:T(8,128)} %bitcast.201, f32[1,512,1024]{2,1,0:T(8,128)} %bitcast.200, f32[1,512,1024]{2,1,0:T(8,128)} %bitcast.197, f32[1,512,1024]{2,1,0:T(8,128)S(1)} %bitcast.195, f32[4,512,512]{2,1,0:T(8,128)} %get-tuple-element.70, f32[4,512,512]{2,1,0:T(8,128)} %get-tuple-element.69), kind=kOutput, calls=%fused_computation.5 | convolution fusion | flops 6450839552 | bytes 20971520 | tf_op jit(solution)/shard_map/pjk,pmk->pjm/dot_general | solution.py:131
  112.3 5.4 %copy.68 = f32[4,512,2,256]{3,0,2,1:T(4,128)} copy(f32[4,512,2,256]{1,3,2,0:T(8,128)} %bitcast.174) | data formatting | bytes 8388608 | tf_op jit(solution)/shard_map/reshape | solution.py:132
  117.7 64.3 %all-to-all-done.1 = f32[512,2,4,256]{3,2,1,0:T(4,128)} async-done(((f32[512,2,4,256]{3,2,1,0:T(4,128)}), f32[512,2,4,256]{3,2,1,0:T(4,128)}, u32[]{:S(2)}, u32[]{:S(2)}) %all-to-all-start.1) | async-done | bytes 4194336 | tf_op jit(solution)/shard_map/all_to_all | solution.py:133
  182.0 6.4 %all-to-all-start = ((f32[512,2,4,256]{3,2,1,0:T(4,128)}), f32[512,2,4,256]{3,2,1,0:T(4,128)}, u32[]{:S(2)}, u32[]{:S(2)}) async-start(f32[512,2,4,256]{3,2,1,0:T(4,128)} %bitcast.170), calls=%async_computation | async-start | bytes 8388608 | tf_op jit(solution)/shard_map/all_to_all | solution.py:133
  188.5 1.0 sort.17
  189.4 0.7 fusion.84
  205.1 5.4 %fusion.22 = (f32[2,8,64,1024]{3,2,1,0:T(8,128)S(1)}, f32[2,8,64,1024]{3,2,1,0:T(8,128)}, f32[2,8,64,1024]{3,2,1,0:T(8,128)}, f32[2,8,64,1024]{3,2,1,0:T(8,128)}) fusion(f32[2,8,64]{2,1,0:T(8,128)S(1)} %copy-done.21, f32[64,1024]{1,0:T(8,128)S(1)} %bitcast.202, f32[2,8,1024]{2,1,0:T(8,128)S(1)} %bitcast.206, f32[64,1024]{1,0:T(8,128)S(1)} %bitcast.203, ...), kind=kLoop, calls=%fused_computation.42 | loop fusion | flops 10485760 | bytes 17444864 | tf_op jit(solution)/shard_map/mul | solution.py:55
  210.5 7.5 %maximum_bitcast_fusion = (f32[2,8,1,64,2048]{4,3,2,1,0:T(8,128)S(1)}, f32[2,8,1,64,2048]{4,3,2,1,0:T(8,128)}) fusion(f32[2,8,64,1024]{3,2,1,0:T(8,128)} %get-tuple-element.80, f32[2,8,64,1024]{3,2,1,0:T(8,128)} %get-tuple-element.82, f32[2,8,64,1024]{3,2,1,0:T(8,128)S(1)} %get-tuple-element.79, f32[2,8,64,1024]{3,2,1,0:T(8,128)} %get-tuple-element.81), kind=kLoop, calls=%fused_computation.13 | loop fusion | flops 4194304 | bytes 33554432 | tf_op jit(solution)/shard_map/stack | solution.py:56
  218.0 8.8 %pad_maximum_fusion = (f32[1,8,2,64,2048]{4,3,2,1,0:T(8,128)}, f32[1,8,2,64,2048]{4,3,2,1,0:T(8,128)}) fusion(f32[2,8,1,64,2048]{4,3,2,1,0:T(8,128)} %get-tuple-element.116, f32[2,8,1,64,2048]{4,3,2,1,0:T(8,128)S(1)} %get-tuple-element.115), kind=kLoop, calls=%fused_computation.3 | loop fusion | flops 4194304 | bytes 33554432 | tf_op jit(solution)/shard_map/stack | solution.py:56
  226.7 6.2 %reshape.437 = f32[8,4,16,2,4,2,128]{6,5,4,3,2,1,0:T(2,128)} reshape(f32[512,2,4,256]{3,2,1,0:T(4,128)} %all-to-all-done.1) | data formatting | bytes 8388608 | tf_op jit(solution)/shard_map/reshape | solution.py:134
  232.9 6.6 %copy.82 = f32[4,2,2,16,4,8,128]{6,5,4,3,1,0,2:T(8,128)} copy(f32[4,2,2,16,4,8,128]{6,2,4,1,3,0,5:T(2,128)} %bitcast.172) | data formatting | bytes 8388608 | tf_op jit(solution)/shard_map/transpose | solution.py:135
  239.6 4.9 %reshape.433 = f32[8,2,64,1024]{3,2,0,1:T(8,128)} reshape(f32[4,2,2,16,4,8,128]{6,5,4,3,1,0,2:T(8,128)} %copy.82) | data formatting | bytes 8388608 | tf_op jit(solution)/shard_map/reshape | solution.py:135
  244.5 37.4 %all-to-all-done = f32[512,2,4,256]{3,2,1,0:T(4,128)} async-done(((f32[512,2,4,256]{3,2,1,0:T(4,128)}), f32[512,2,4,256]{3,2,1,0:T(4,128)}, u32[]{:S(2)}, u32[]{:S(2)}) %all-to-all-start) | async-done | bytes 4194336 | tf_op jit(solution)/shard_map/all_to_all | solution.py:133
  281.8 6.2 %reshape.436 = f32[8,4,16,2,4,2,128]{6,5,4,3,2,1,0:T(2,128)} reshape(f32[512,2,4,256]{3,2,1,0:T(4,128)} %all-to-all-done) | data formatting | bytes 8388608 | tf_op jit(solution)/shard_map/reshape | solution.py:134
  288.1 6.6 %copy.70 = f32[4,2,2,16,4,8,128]{6,5,4,3,1,0,2:T(8,128)} copy(f32[4,2,2,16,4,8,128]{6,2,4,1,3,0,5:T(2,128)} %bitcast.173) | data formatting | bytes 8388608 | tf_op jit(solution)/shard_map/transpose | solution.py:135
  294.7 5.0 %reshape.422 = f32[8,2,64,1024]{3,2,0,1:T(8,128)} reshape(f32[4,2,2,16,4,8,128]{6,5,4,3,1,0,2:T(8,128)} %copy.70) | data formatting | bytes 8388608 | tf_op jit(solution)/shard_map/reshape | solution.py:135
  299.8 1.2 dynamic-slice_dynamic-update-slice_fusion.15
  301.0 1.7 dynamic-slice_dynamic-update-slice_fusion.7
  302.7 1.8 dynamic-slice_dynamic-update-slice_fusion.14
  304.6 1.1 dynamic-slice_dynamic-update-slice_fusion.6
  305.6 1.1 dynamic-slice_dynamic-update-slice_fusion.13
  306.8 1.1 dynamic-slice_dynamic-update-slice_fusion.12
  308.4 2.0 copy-done.9
  310.4 1.8 slice-done.1
  312.2 7.4 %fusion.28 = f32[8,64,2048]{2,1,0:T(8,128)S(1)} fusion(f32[1024,2048,1]{1,0,2:T(8,128)S(1)} %bitcast.164, f32[8,2,64,1024]{3,2,0,1:T(8,128)S(1)} %dynamic-slice_dynamic-update-slice_fusion), kind=kOutput, calls=%fused_computation.49 | convolution fusion | flops 6442450944 | bytes 14680064 | tf_op jit(solution)/shard_map/lyk,kx->lyx/dot_general | solution.py:142
  319.7 7.7 %fusion.30 = f32[8,64,2048]{2,1,0:T(8,128)S(1)} fusion(f32[1024,2048,1]{1,0,2:T(8,128)S(1)} %bitcast.165, f32[8,2,64,1024]{3,2,0,1:T(8,128)S(1)} %dynamic-slice_dynamic-update-slice_fusion.8), kind=kOutput, calls=%fused_computation.53 | convolution fusion | flops 6442450944 | bytes 14680064 | tf_op jit(solution)/shard_map/lyk,kx->lyx/dot_general | solution.py:142
  327.4 11.6 %fusion.79 = (f32[8,64,2048]{2,1,0:T(8,128)}, f32[8,64,2048]{2,1,0:T(8,128)S(1)}) fusion(f32[8,64,2048]{2,1,0:T(8,128)S(1)} %fusion.30, f32[1024,2048,1]{1,0,2:T(8,128)S(1)} %bitcast.168, f32[8,2,64,1024]{3,2,0,1:T(8,128)} %copy-done.10), kind=kOutput, calls=%fused_computation.165 | convolution fusion | flops 6444548096 | bytes 23068672 | tf_op jit(solution)/shard_map/lyk,kx->lyx/dot_general | solution.py:141
  339.0 11.6 %fusion.78 = (f32[8,64,2048]{2,1,0:T(8,128)}, f32[8,64,2048]{2,1,0:T(8,128)S(1)}) fusion(f32[8,64,2048]{2,1,0:T(8,128)S(1)} %fusion.28, f32[1024,2048,1]{1,0,2:T(8,128)S(1)} %bitcast.169, f32[8,2,64,1024]{3,2,0,1:T(8,128)} %copy-done.9), kind=kOutput, calls=%fused_computation.164 | convolution fusion | flops 6444548096 | bytes 23068672 | tf_op jit(solution)/shard_map/lyk,kx->lyx/dot_general | solution.py:141
  350.6 2.9 fusion.82
  353.5 0.6 copy-done.8
  354.4 0.6 fusion.83
  354.9 0.6 fusion.81
  355.5 2.5 pad_maximum_fusion.6
  358.0 2.5 pad_maximum_fusion.4
  360.6 2.5 pad_maximum_fusion.7
  363.1 2.5 pad_maximum_fusion.5
  (83 shorter events, 4.6 us)
Async XLA Ops:
  10.7 30.4 %copy-start.1 = (f32[2,2,64,2048]{3,2,1,0:T(8,128)}, f32[2,2,64,2048]{3,2,1,0:T(8,128)S(1)}, u32[]{:S(2)}) copy-start(f32[2,2,64,2048]{3,2,1,0:T(8,128)S(1)} %slice.167) | copy-start | bytes 6291460
  40.4 1.6 copy-start.3
  40.4 2.2 copy-start.4
  42.6 2.2 copy-start.5
  44.6 1.6 copy-start.2
  55.4 1.8 copy-start.19
  55.4 1.9 copy-start.18
  55.4 2.0 copy-start.14
  55.4 2.0 copy-start.15
  82.0 99.9 %all-to-all-start.1 = ((f32[512,2,4,256]{3,2,1,0:T(4,128)}), f32[512,2,4,256]{3,2,1,0:T(4,128)}, u32[]{:S(2)}, u32[]{:S(2)}) async-start(f32[512,2,4,256]{3,2,1,0:T(4,128)} %bitcast.171), calls=%async_computation.1 | async-start | bytes 8388608 | tf_op jit(solution)/shard_map/all_to_all | solution.py:133
  88.5 1.6 copy-start
  96.2 2.1 copy-start.11
  182.0 6.5 %copy-start.23 = (s32[8]{0:T(128)S(1)}, s32[8]{0:T(128)}, u32[]{:S(2)}) copy-start(s32[8]{0:T(128)} %param.19) | copy-start | bytes 100
  182.0 23.1 %copy-start.12 = (f32[1,1,64,1024]{3,2,1,0:T(8,128)S(1)}, f32[1,1,64,1024]{3,2,1,0:T(8,128)}, u32[]{:S(2)}) copy-start(f32[1,1,64,1024]{3,2,1,0:T(8,128)} %constant.55.clone) | copy-start | bytes 786436
  182.0 23.1 %copy-start.13 = (f32[1,1,64,1024]{3,2,1,0:T(8,128)S(1)}, f32[1,1,64,1024]{3,2,1,0:T(8,128)}, u32[]{:S(2)}) copy-start(f32[1,1,64,1024]{3,2,1,0:T(8,128)} %constant.54.clone) | copy-start | bytes 786436
  182.0 23.1 %copy-start.16 = (f32[2,8,1,1024]{3,1,0,2:T(8,128)S(1)}, f32[2,8,1,1024]{3,1,0,2:T(8,128)}, u32[]{:S(2)}) copy-start(f32[2,8,1,1024]{3,1,0,2:T(8,128)} %constant.53.clone) | copy-start | bytes 196612
  182.0 23.1 %copy-start.17 = (f32[2,8,1,1024]{3,1,0,2:T(8,128)S(1)}, f32[2,8,1,1024]{3,1,0,2:T(8,128)}, u32[]{:S(2)}) copy-start(f32[2,8,1,1024]{3,1,0,2:T(8,128)} %constant.52.clone) | copy-start | bytes 196612
  182.0 23.1 %copy-start.20 = (f32[2,8,64]{2,1,0:T(8,128)S(1)}, f32[2,8,64]{2,1,0:T(8,128)}, u32[]{:S(2)}) copy-start(f32[2,8,64]{2,1,0:T(8,128)} %constant.63) | copy-start | bytes 12292
  182.0 23.1 %copy-start.21 = (f32[2,8,64]{2,1,0:T(8,128)S(1)}, f32[2,8,64]{2,1,0:T(8,128)}, u32[]{:S(2)}) copy-start(f32[2,8,64]{2,1,0:T(8,128)} %constant.62) | copy-start | bytes 12292
  182.0 23.1 %copy-start.22 = (f32[2,8,64]{2,1,0:T(8,128)S(1)}, f32[2,8,64]{2,1,0:T(8,128)}, u32[]{:S(2)}) copy-start(f32[2,8,64]{2,1,0:T(8,128)} %constant.61) | copy-start | bytes 12292
  182.0 99.8 %all-to-all-start = ((f32[512,2,4,256]{3,2,1,0:T(4,128)}), f32[512,2,4,256]{3,2,1,0:T(4,128)}, u32[]{:S(2)}, u32[]{:S(2)}) async-start(f32[512,2,4,256]{3,2,1,0:T(4,128)} %bitcast.170), calls=%async_computation | async-start | bytes 8388608 | tf_op jit(solution)/shard_map/all_to_all | solution.py:133
  299.7 7.0 %copy-start.6 = (f32[8,2,64,1024]{3,2,0,1:T(8,128)S(1)}, f32[8,2,64,1024]{3,2,0,1:T(8,128)}, u32[]{:S(2)}) copy-start(f32[8,2,64,1024]{3,2,0,1:T(8,128)} %reshape.433) | copy-start | bytes 12582916
  299.7 8.2 %copy-start.7 = (f32[8,2,64,1024]{3,2,0,1:T(8,128)S(1)}, f32[8,2,64,1024]{3,2,0,1:T(8,128)}, u32[]{:S(2)}) copy-start(f32[8,2,64,1024]{3,2,0,1:T(8,128)} %reshape.422) | copy-start | bytes 12582916
  301.0 9.4 %slice-start = ((s8[8388608]{0:T(1024)(128)(4,1)}), s8[4194304]{0:T(1024)(128)(4,1)S(1)}, s32[]{:S(2)}) async-start(s8[8388608]{0:T(1024)(128)(4,1)} %bitcast.162), calls=%async_computation.2 | async-start | bytes 8388608
  308.0 4.3 %slice-start.1 = ((s8[8388608]{0:T(1024)(128)(4,1)}), s8[4194304]{0:T(1024)(128)(4,1)S(1)}, s32[]{:S(2)}) async-start(s8[8388608]{0:T(1024)(128)(4,1)} %bitcast.162), calls=%async_computation.3 | async-start | bytes 8388608
  308.3 19.0 %copy-start.10 = (f32[8,2,64,1024]{3,2,0,1:T(8,128)}, f32[8,2,64,1024]{3,2,0,1:T(8,128)S(1)}, u32[]{:S(2)}) copy-start(f32[8,2,64,1024]{3,2,0,1:T(8,128)S(1)} %dynamic-slice_dynamic-update-slice_fusion.8) | copy-start | bytes 12582916
  308.4 2.0 copy-start.9
  312.2 15.1 %slice-start.2 = ((s8[8388608]{0:T(1024)(128)(4,1)}), s8[4194304]{0:T(1024)(128)(4,1)S(1)}, s32[]{:S(2)}) async-start(s8[8388608]{0:T(1024)(128)(4,1)} %bitcast.166), calls=%async_computation.4 | async-start | bytes 8388608
  319.7 7.7 %slice-start.3 = ((s8[8388608]{0:T(1024)(128)(4,1)}), s8[4194304]{0:T(1024)(128)(4,1)S(1)}, s32[]{:S(2)}) async-start(s8[8388608]{0:T(1024)(128)(4,1)} %bitcast.166), calls=%async_computation.5 | async-start | bytes 8388608
  350.6 3.4 copy-start.8
